TPU v7x, 32 devices: a whole 2x2x4 slice. The times are simulated.
32 devices in a mesh: section: 4 (over z), space: 8 (over y, x, core).
Axes of the slice: x: 2, y: 2, z: 4, core: 2. Of those that a mesh axis runs over, the one named last changes fastest.
Arguments:
- features: bfloat16 [1, 32, 128, 320], P(None, 'space'), may hold values from -30 to 30
- section_packs: bfloat16 [4, 11520, 640], P('section', None, 'space'), may hold values from -6 to 6
Outputs:
- output: bfloat16 [1, 32, 128, 320], P(None, 'space', 'section')
All inputs are finite; a program needn't handle non-finite values.
Results may differ from a plain program's by a relative error of at most 0.009.
Values may be sent and summed in bfloat16 or wider, within the bound.
No kernel may reach another device: no remote copies, remote signals or barrier semaphores. Data moves between devices by JAX's collectives and lax.ppermute only.
A program may use at most 128 MiB of HBM per device.

v0:
```python
from functools import partial
import math
import jax
import jax.numpy as jnp
from jax import lax
from jax.sharding import PartitionSpec as P

GROUPS = 32
EPSILON = 1e-05


def for_sending(x):
    return jax.tree.map(lambda a: a.astype(jnp.bfloat16) if a.dtype == jnp.float32 else a, x)


def padded(x, sides, width):
    for axis, dim in sides:
        size, length = (lax.axis_size(axis), x.shape[dim])
        up = [(i, (i + 1) % size) for i in range(size - 1)]
        down = [(j, i) for i, j in up]
        last = lax.slice_in_dim(x, length - width, length, axis=dim)
        initial = lax.slice_in_dim(x, 0, width, axis=dim)
        before = lax.ppermute(last, axis, up)
        after = lax.ppermute(initial, axis, down)
        x = jnp.concatenate([before, x, after], axis=dim)
    return x


def passed_along(value, axis, steps):
    count = lax.axis_size(axis)
    initial, last = (max(0, -steps), min(count, count - steps))
    return lax.ppermute(value, axis, [(source, source + steps) for source in range(initial, last)])


def convolve_rows(field_ext, kernel, fan_in, stride):
    result = lax.conv_general_dilated(
        field_ext[None],
        kernel,
        (stride, stride),
        ((0, 0), (1, 1)),
        dimension_numbers=("NHWC", "HWIO", "NHWC"),
        preferred_element_type=jnp.float32,
    )[0]
    return result * (1.0 / math.sqrt(fan_in))


def kernel_at(flat_pack, offset, c_in, c_out):
    return flat_pack[offset : offset + 9 * c_in * c_out].reshape(3, 3, c_in, c_out)


def grouped_view(values):
    return values.reshape(-1, GROUPS, values.shape[-1] // GROUPS)


def normalize(values, group_mean, group_var):
    shape_in = values.shape
    grouped = values.reshape(shape_in[:-1] + (GROUPS, shape_in[-1] // GROUPS))
    normed = (grouped - group_mean[:, None]) / jnp.sqrt(group_var + EPSILON)[:, None]
    return normed.reshape(shape_in)


def activate_ext(raw_ext, group_mean, group_var, top_edge, bottom_edge, ghost_rows):
    activated = jax.nn.silu(normalize(raw_ext.astype(jnp.float32), group_mean, group_var))
    row_ids = lax.broadcasted_iota(jnp.int32, (raw_ext.shape[0], 1, 1), 0)
    dropped = (row_ids < ghost_rows) & top_edge | (
        row_ids >= raw_ext.shape[0] - ghost_rows
    ) & bottom_edge
    return jnp.where(dropped, 0.0, activated).astype(jnp.bfloat16)


def edge_rows(block, ghost_rows):
    return jnp.concatenate(
        [
            block[:ghost_rows].reshape(ghost_rows, -1),
            block[block.shape[0] - ghost_rows :].reshape(ghost_rows, -1),
        ],
        0,
    )


def add_rows(cycle_rows, block, ghost_rows):
    row_shape = (ghost_rows,) + block.shape[1:]
    return jnp.concatenate(
        [
            cycle_rows[:ghost_rows].reshape(row_shape),
            block,
            cycle_rows[3 * ghost_rows :].reshape(row_shape),
        ],
        0,
    )


def trim_rows(block, count):
    return block[count : block.shape[0] - count]


def branches(func):
    return [
        partial(func, 0),
        partial(func, 1),
        partial(func, 2),
        partial(func, 3),
        partial(func, 4),
    ]


def shards(features, section_packs):
    section_id = lax.axis_index("section")
    row_dev = lax.axis_index("space")
    n_space = lax.axis_size("space")
    top_edge = row_dev == 0
    bottom_edge = row_dev == n_space - 1
    micro_count, fine_rows, fine_cols, narrow = features.shape
    wide_ch = 2 * narrow
    square = narrow * narrow
    fine_shape = (fine_rows, fine_cols, narrow)
    coarse_shape = (fine_rows // 2, fine_cols // 2, wide_ch)
    fine_zero = jnp.zeros(fine_shape, jnp.bfloat16)
    coarse_zero = jnp.zeros(coarse_shape, jnp.bfloat16)
    is_fine = (section_id == 0) | (section_id == 3)
    gathered = lax.all_gather(section_packs, "space", axis=2, tiled=True)
    flat_pack = gathered.reshape(-1)
    ghost_rows = 1

    def row_rims(block_rims):
        return padded(for_sending(block_rims), (("space", 0),), 1).astype(block_rims.dtype)

    spare = ghost_rows - 1
    fine_hidden_zero = jnp.zeros((fine_rows + 2 * spare, fine_cols, narrow), jnp.bfloat16)
    coarse_hidden_zero = jnp.zeros(
        (fine_rows // 2 + 2 * spare, fine_cols // 2, wide_ch), jnp.bfloat16
    )

    def moments(branch_pick, source):
        empty = jnp.zeros((GROUPS,), jnp.float32)

        def pair_sums(branch_id):
            if branch_id == 4:
                return (empty, empty)
            grouped = grouped_view(source(branch_id))
            factor = 1.0 / (grouped.shape[0] * grouped.shape[2] * n_space)
            return (
                jnp.sum(grouped, axis=(0, 2)) * factor,
                jnp.sum(jnp.square(grouped), axis=(0, 2)) * factor,
            )

        first_part, second_part = lax.switch(branch_pick, branches(pair_sums))
        group_mean, mean_square = lax.psum((first_part, second_part), "space")
        return (group_mean, mean_square - group_mean * group_mean)

    def section_tick(tick_id, loop_state):
        handoff, skip_store, results = loop_state
        micro_id = tick_id - section_id
        active = (micro_id >= 0) & (micro_id < micro_count)
        micro_slot = jnp.clip(micro_id, 0, micro_count - 1)
        branch_pick = jnp.where(active, section_id, 4)
        skip_ext = lax.dynamic_index_in_dim(skip_store, micro_slot, 0, keepdims=False)
        skip_inner = trim_rows(skip_ext, ghost_rows)
        cycle_in = row_rims(edge_rows(handoff, ghost_rows))

        def section_entry(branch_id):
            if branch_id == 0:
                return (
                    lax.dynamic_index_in_dim(features, micro_slot, 0, keepdims=False),
                    coarse_zero,
                )
            if branch_id == 3:
                coarse_ext = trim_rows(add_rows(cycle_in, handoff, ghost_rows), spare)
                upsampled = jnp.repeat(jnp.repeat(coarse_ext, 2, 0), 2, 1)[1:-1]
                made = convolve_rows(
                    upsampled, kernel_at(flat_pack, 0, wide_ch, narrow), 9 * wide_ch, 1
                )
                return (made.astype(jnp.bfloat16), coarse_zero)
            if branch_id == 4:
                return (fine_zero, coarse_zero)
            return (fine_zero, handoff)

        fine_in, coarse_in = lax.switch(branch_pick, branches(section_entry))

        def block_input(branch_id):
            if branch_id == 0:
                return fine_in.astype(jnp.float32)
            if branch_id == 3:
                return jnp.concatenate([fine_in, skip_inner], -1).astype(jnp.float32)
            return coarse_in.astype(jnp.float32)

        mean_one, var_one = moments(branch_pick, block_input)
        cycle_one = row_rims(
            jnp.where(is_fine, edge_rows(fine_in, ghost_rows), edge_rows(coarse_in, ghost_rows))
        )

        def first_conv(branch_id):
            if branch_id == 4:
                return (fine_hidden_zero, coarse_hidden_zero)
            if branch_id in (1, 2):
                activated = activate_ext(
                    add_rows(cycle_one, coarse_in, ghost_rows),
                    mean_one,
                    var_one,
                    top_edge,
                    bottom_edge,
                    ghost_rows,
                )
                made = convolve_rows(
                    activated, kernel_at(flat_pack, 0, wide_ch, wide_ch), 9 * wide_ch, 1
                )
                return (fine_hidden_zero, made.astype(jnp.bfloat16))
            raw_ext = add_rows(cycle_one, fine_in, ghost_rows)
            c_in = narrow
            offset = 0
            if branch_id == 3:
                raw_ext = jnp.concatenate([raw_ext, skip_ext], -1)
                c_in = wide_ch
                offset = 18 * square
            activated = activate_ext(raw_ext, mean_one, var_one, top_edge, bottom_edge, ghost_rows)
            made = convolve_rows(activated, kernel_at(flat_pack, offset, c_in, narrow), 9 * c_in, 1)
            return (made.astype(jnp.bfloat16), coarse_hidden_zero)

        hidden_fine, hidden_coarse = lax.switch(branch_pick, branches(first_conv))

        def hidden_input(branch_id):
            if branch_id in (0, 3):
                return trim_rows(hidden_fine, spare).astype(jnp.float32)
            return trim_rows(hidden_coarse, spare).astype(jnp.float32)

        mean_two, var_two = moments(branch_pick, hidden_input)
        cycle_two = row_rims(
            jnp.where(is_fine, edge_rows(hidden_fine, 1), edge_rows(hidden_coarse, 1))
        )
        fine_hidden_ext = add_rows(cycle_two, hidden_fine, 1)
        coarse_hidden_ext = add_rows(cycle_two, hidden_coarse, 1)

        def second_conv(branch_id):
            if branch_id == 4:
                return (fine_zero, coarse_zero)
            if branch_id in (1, 2):
                activated = activate_ext(
                    coarse_hidden_ext, mean_two, var_two, top_edge, bottom_edge, 1
                )
                update = convolve_rows(
                    activated, kernel_at(flat_pack, 36 * square, wide_ch, wide_ch), 9 * wide_ch, 1
                )
                return (fine_zero, (coarse_in.astype(jnp.float32) + update).astype(jnp.bfloat16))
            activated = activate_ext(fine_hidden_ext, mean_two, var_two, top_edge, bottom_edge, 1)
            if branch_id == 0:
                update = convolve_rows(
                    activated, kernel_at(flat_pack, 9 * square, narrow, narrow), 9 * narrow, 1
                )
                return ((fine_in.astype(jnp.float32) + update).astype(jnp.bfloat16), coarse_zero)
            update = convolve_rows(
                activated, kernel_at(flat_pack, 36 * square, narrow, narrow), 9 * narrow, 1
            )
            joined = jnp.concatenate([fine_in, skip_inner], -1)
            projection = jnp.dot(
                joined.reshape(-1, wide_ch),
                flat_pack[45 * square : 47 * square].reshape(wide_ch, narrow),
                preferred_element_type=jnp.float32,
            )
            projection = projection.reshape(fine_shape) * (1.0 / math.sqrt(wide_ch))
            return ((projection + update).astype(jnp.bfloat16), coarse_zero)

        out_fine, out_coarse = lax.switch(branch_pick, branches(second_conv))
        cycle_three = row_rims(edge_rows(out_fine, ghost_rows))
        made_skip = add_rows(cycle_three, out_fine, ghost_rows)

        def section_exit(branch_id):
            if branch_id == 0:
                made = convolve_rows(
                    trim_rows(made_skip, spare),
                    kernel_at(flat_pack, 18 * square, narrow, wide_ch),
                    9 * narrow,
                    2,
                )
                return made.astype(jnp.bfloat16)
            if branch_id in (1, 2):
                return out_coarse
            return coarse_zero

        coarse_out = lax.switch(branch_pick, branches(section_exit))
        next_handoff = jax.tree.map(
            lambda part, own: part.astype(own.dtype),
            passed_along(for_sending(coarse_out), "section", 1),
            coarse_out,
        )
        incoming = passed_along(for_sending(made_skip), "section", 3).astype(made_skip.dtype)
        store_here = (section_id == 3) & (tick_id < micro_count)
        store_slot = jnp.clip(tick_id, 0, micro_count - 1)
        current = lax.dynamic_index_in_dim(skip_store, store_slot, 0, keepdims=False)
        skip_store = lax.dynamic_update_index_in_dim(
            skip_store, jnp.where(store_here, incoming, current), store_slot, 0
        )
        result_now = lax.dynamic_index_in_dim(results, micro_slot, 0, keepdims=False)
        results = lax.dynamic_update_index_in_dim(
            results, jnp.where((section_id == 3) & active, out_fine, result_now), micro_slot, 0
        )
        return (next_handoff, skip_store, results)

    skip_start = jnp.zeros(
        (micro_count, fine_rows + 2 * ghost_rows, fine_cols, narrow), jnp.bfloat16
    )
    result_start = jnp.zeros((micro_count,) + fine_shape, jnp.bfloat16)
    final_state = lax.fori_loop(
        0, micro_count + 3, section_tick, (coarse_zero, skip_start, result_start)
    )
    results = final_state[2]
    return lax.psum_scatter(
        results.astype(jnp.float32).astype(jnp.bfloat16), "section", scatter_dimension=2, tiled=True
    )


def solution(mesh):
    return jax.shard_map(
        shards,
        mesh=mesh,
        in_specs=(P(None, "space", None, None), P("section", None, "space")),
        out_specs=P(None, "space", "section", None),
        check_vma=False,
    )
```

profile of v0, /device:TPU:0, one launch (start us, length us, event | category | flops | bytes accessed | tf_op | source)
XLA Modules:
  0.0 817.5 jit_solution(6047263199579071338)
XLA Ops:
  7.3 85.8 %all-gather.2.cloned.1.call-done = bf16[1,11520,640]{1,2,0:T(8,128)(2,1)} async-done(((bf16[1,11520,80]{1,2,0:T(8,128)(2,1)}), bf16[1,11520,640]{1,2,0:T(8,128)(2,1)}) %all-gather.2.cloned.1.call-update) | async-done | bytes 14745616 | tf_op jit(solution)/shard_map/all_gather | solution.py:121
  93.1 18.7 %copy.218 = bf16[1,11520,640]{2,1,0:T(8,128)(2,1)} copy(bf16[1,11520,640]{1,2,0:T(8,128)(2,1)} %all-gather.2.cloned.1.call-done) | data formatting | bytes 29491200 | tf_op jit(solution)/shard_map/all_gather | solution.py:121
  111.8 24.4 %reshape.795 = bf16[7372800]{0:T(1024)(128)(2,1)} reshape(bf16[1,11520,640]{2,1,0:T(8,128)(2,1)} %copy.218) | data formatting | bytes 29491200 | tf_op jit(solution)/shard_map/reshape | solution.py:122
  137.2 641.9 %while.24 = (s32[]{:T(128)}, bf16[2,64,640]{2,0,1:T(2,128)(2,1)S(1)}, bf16[1,6,128,320]{2,3,1,0:T(8,128)(2,1)S(1)}, bf16[1,4,128,320]{2,3,1,0:T(8,128)(2,1)}, s3...) while((s32[]{:T(128)}, ...), condition=%wide.region_67.68_spmd, body=%wide.region_0.67_spmd.sunk | while | flops 5784842240 | bytes 176676080 | solution.py:302
  139.1 3.0 collective-permute-start
  143.1 4.8 conditional.12
  150.6 2.2 collective-permute-start.2
  154.7 15.0 %all-reduce.4 = (f32[32]{0:T(128)S(1)}, f32[32]{0:T(128)S(1)}) all-reduce(f32[32]{0:T(128)S(1)} %get-tuple-element.957, f32[32]{0:T(128)S(1)} %get-tuple-element.958), channel_id=1, replica_groups=mesh['section'=4,'space'=8] {'space'}, use_global_device_ids=true, to_apply=%region_27.27 | all-reduce | flops 64 | bytes 512 | tf_op jit(solution)/shard_map/while/body/eval_jaxpr/psum | solution.py:148
  169.7 27.9 %conditional.14 = (bf16[4,128,320]{2,0,1:T(4,128)(2,1)S(1)}, bf16[2,64,640]{2,1,0:T(8,128)(2,1)}, bf16[2,64,640]{2,0,1:T(2,128)(2,1)}, bf16[1,40960]{1,0:T(2,128)(2,1)S(1)}, bf16[1,40960]{1,0:T(2,128)(2,1)S(1)}) conditional(s32[]{:T(128)} %clamp.14, (pred[]{:T(512)}, pred[]{:T(512)}, bf16[1,40960]{1,0:T(2,128)(2,1)S(1)}, ...), branch_computations={%region_29.29_spmd.clone, %region_30.30_spmd.clone, %region_31.31_... | conditional | flops 2017290240 | bytes 48206080 | solution.py:219
  170.5 1.7 slice.311
  173.8 3.1 reshape.944
  178.2 3.4 fusion.129
  203.1 3.0 collective-permute-done.5
  207.5 17.3 %all-reduce.5 = (f32[32]{0:T(128)S(1)}, f32[32]{0:T(128)S(1)}) all-reduce(f32[32]{0:T(128)S(1)} %get-tuple-element.971, f32[32]{0:T(128)S(1)} %get-tuple-element.972), channel_id=1, replica_groups=mesh['section'=4,'space'=8] {'space'}, use_global_device_ids=true, to_apply=%region_55.55 | all-reduce | flops 64 | bytes 512 | tf_op jit(solution)/shard_map/while/body/eval_jaxpr/psum | solution.py:148
  224.9 2.2 pad_maximum_fusion.6
  227.1 19.0 %conditional.16 = (bf16[4,128,320]{1,2,0:T(8,128)(2,1)S(1)}, bf16[2,64,640]{2,1,0:T(8,128)(2,1)S(1)}) conditional(s32[]{:T(128)} %clamp.14, (bf16[4,128,320]{2,0,1:T(4,128)(2,1)S(1)}, pred[]{:T(512)}, pred[]{:T(512)}, bf16[6,128,320]{2,1,0:T(8,128)(2,1)S(1)}, f32[32]{0:T(128)S(1)}, /*index=5*/f32[32]{0:T(128)S(1)}, ...), branch_computations={%region_57.57_spmd, %region_58.58_spmd, %region_59.59_spmd, %regio... | conditional | flops 1218529280 | bytes 43285440 | solution.py:262
  230.1 3.1 reshape.774
  233.1 3.5 fusion.9
  250.1 2.8 collective-permute-done.6
  254.5 2.1 collective-permute-start.9
  257.4 16.4 %conditional.17 = (bf16[2,64,640]{2,0,1:T(2,128)(2,1)S(1)}) conditional(s32[]{:T(128)} %clamp.14, (bf16[6,128,320]{1,2,0:T(8,128)(2,1)}, bf16[7372800]{0:T(1024)(128)(2,1)}) %tuple.329, bf16[2,64,640]{2,1,0:T(8,128)(2,1)S(1)} %get-tuple-element.979, bf16[2,64,640]{2,1,0:T(8,128)(2,1)S(1)} %get-tuple-element.979, ...), branch_computations={%region_62.62_spmd, %region_63.63_spmd, %region_64.64_spmd, %regio... | conditional | flops 532961280 | bytes 24266638 | solution.py:279
  257.5 3.4 slice.261
  261.0 7.2 slice.262
  270.4 2.9 fusion.75
  275.2 2.7 collective-permute-done.8
  282.2 7.6 collective-permute-start
  293.9 6.7 collective-permute-start.2
  302.0 15.4 %all-reduce.4 = (f32[32]{0:T(128)S(1)}, f32[32]{0:T(128)S(1)}) all-reduce(f32[32]{0:T(128)S(1)} %get-tuple-element.957, f32[32]{0:T(128)S(1)} %get-tuple-element.958), channel_id=1, replica_groups=mesh['section'=4,'space'=8] {'space'}, use_global_device_ids=true, to_apply=%region_27.27 | all-reduce | flops 64 | bytes 512 | tf_op jit(solution)/shard_map/while/body/eval_jaxpr/psum | solution.py:148
  317.4 15.1 %conditional.14 = (bf16[4,128,320]{2,0,1:T(4,128)(2,1)S(1)}, bf16[2,64,640]{2,1,0:T(8,128)(2,1)}, bf16[2,64,640]{2,0,1:T(2,128)(2,1)}, bf16[1,40960]{1,0:T(2,128)(2,1)S(1)}, bf16[1,40960]{1,0:T(2,128)(2,1)S(1)}) conditional(s32[]{:T(128)} %clamp.14, (pred[]{:T(512)}, pred[]{:T(512)}, bf16[1,40960]{1,0:T(2,128)(2,1)S(1)}, ...), branch_computations={%region_29.29_spmd.clone, %region_30.30_spmd.clone, %region_31.31_... | conditional | flops 2017290240 | bytes 48206080 | solution.py:219
  334.8 1.8 collective-permute-start.4
  338.6 3.1 collective-permute-done.5
  342.6 17.7 %all-reduce.5 = (f32[32]{0:T(128)S(1)}, f32[32]{0:T(128)S(1)}) all-reduce(f32[32]{0:T(128)S(1)} %get-tuple-element.971, f32[32]{0:T(128)S(1)} %get-tuple-element.972), channel_id=1, replica_groups=mesh['section'=4,'space'=8] {'space'}, use_global_device_ids=true, to_apply=%region_55.55 | all-reduce | flops 64 | bytes 512 | tf_op jit(solution)/shard_map/while/body/eval_jaxpr/psum | solution.py:148
  360.3 2.2 pad_maximum_fusion.6
  362.5 8.7 %conditional.16 = (bf16[4,128,320]{1,2,0:T(8,128)(2,1)S(1)}, bf16[2,64,640]{2,1,0:T(8,128)(2,1)S(1)}) conditional(s32[]{:T(128)} %clamp.14, (bf16[4,128,320]{2,0,1:T(4,128)(2,1)S(1)}, pred[]{:T(512)}, pred[]{:T(512)}, bf16[6,128,320]{2,1,0:T(8,128)(2,1)S(1)}, f32[32]{0:T(128)S(1)}, /*index=5*/f32[32]{0:T(128)S(1)}, ...), branch_computations={%region_57.57_spmd, %region_58.58_spmd, %region_59.59_spmd, %regio... | conditional | flops 1218529280 | bytes 43285440 | solution.py:262
  375.2 2.8 collective-permute-done.6
  379.6 2.1 collective-permute-start.9
  384.0 47.7 %collective-permute-start.8 = (bf16[2,64,640]{2,0,1:T(2,128)(2,1)S(1)}, bf16[2,64,640]{2,0,1:T(2,128)(2,1)S(1)}, u32[]{:S(2)}, u32[]{:S(2)}) collective-permute-start(bf16[2,64,640]{2,0,1:T(2,128)(2,1)S(1)} %get-tuple-element.1090), channel_id=1, source_target_pairs={{0,8},{8,16},{16,24},{1,9},{9,17},{17,25},{2,10},{10,18},{18,26},{... | collective-permute-start | bytes 491528 | tf_op jit(solution)/shard_map/while/body/eval_jaxpr/ppermute | solution.py:32
  431.7 2.7 collective-permute-done.8
  436.2 6.8 collective-permute-start
  447.6 6.2 collective-permute-start.2
  455.1 15.6 %all-reduce.4 = (f32[32]{0:T(128)S(1)}, f32[32]{0:T(128)S(1)}) all-reduce(f32[32]{0:T(128)S(1)} %get-tuple-element.957, f32[32]{0:T(128)S(1)} %get-tuple-element.958), channel_id=1, replica_groups=mesh['section'=4,'space'=8] {'space'}, use_global_device_ids=true, to_apply=%region_27.27 | all-reduce | flops 64 | bytes 512 | tf_op jit(solution)/shard_map/while/body/eval_jaxpr/psum | solution.py:148
  470.8 15.1 %conditional.14 = (bf16[4,128,320]{2,0,1:T(4,128)(2,1)S(1)}, bf16[2,64,640]{2,1,0:T(8,128)(2,1)}, bf16[2,64,640]{2,0,1:T(2,128)(2,1)}, bf16[1,40960]{1,0:T(2,128)(2,1)S(1)}, bf16[1,40960]{1,0:T(2,128)(2,1)S(1)}) conditional(s32[]{:T(128)} %clamp.14, (pred[]{:T(512)}, pred[]{:T(512)}, bf16[1,40960]{1,0:T(2,128)(2,1)S(1)}, ...), branch_computations={%region_29.29_spmd.clone, %region_30.30_spmd.clone, %region_31.31_... | conditional | flops 2017290240 | bytes 48206080 | solution.py:219
  491.7 3.1 collective-permute-done.5
  495.7 17.7 %all-reduce.5 = (f32[32]{0:T(128)S(1)}, f32[32]{0:T(128)S(1)}) all-reduce(f32[32]{0:T(128)S(1)} %get-tuple-element.971, f32[32]{0:T(128)S(1)} %get-tuple-element.972), channel_id=1, replica_groups=mesh['section'=4,'space'=8] {'space'}, use_global_device_ids=true, to_apply=%region_55.55 | all-reduce | flops 64 | bytes 512 | tf_op jit(solution)/shard_map/while/body/eval_jaxpr/psum | solution.py:148
  513.4 2.2 pad_maximum_fusion.6
  515.6 8.7 %conditional.16 = (bf16[4,128,320]{1,2,0:T(8,128)(2,1)S(1)}, bf16[2,64,640]{2,1,0:T(8,128)(2,1)S(1)}) conditional(s32[]{:T(128)} %clamp.14, (bf16[4,128,320]{2,0,1:T(4,128)(2,1)S(1)}, pred[]{:T(512)}, pred[]{:T(512)}, bf16[6,128,320]{2,1,0:T(8,128)(2,1)S(1)}, f32[32]{0:T(128)S(1)}, /*index=5*/f32[32]{0:T(128)S(1)}, ...), branch_computations={%region_57.57_spmd, %region_58.58_spmd, %region_59.59_spmd, %regio... | conditional | flops 1218529280 | bytes 43285440 | solution.py:262
  528.3 2.8 collective-permute-done.6
  532.7 2.1 collective-permute-start.9
  537.1 4.1 collective-permute-start.8
  541.6 4.1 collective-permute-done.8
  547.5 6.2 collective-permute-start
  558.9 5.6 collective-permute-start.2
  565.9 17.2 %all-reduce.4 = (f32[32]{0:T(128)S(1)}, f32[32]{0:T(128)S(1)}) all-reduce(f32[32]{0:T(128)S(1)} %get-tuple-element.957, f32[32]{0:T(128)S(1)} %get-tuple-element.958), channel_id=1, replica_groups=mesh['section'=4,'space'=8] {'space'}, use_global_device_ids=true, to_apply=%region_27.27 | all-reduce | flops 64 | bytes 512 | tf_op jit(solution)/shard_map/while/body/eval_jaxpr/psum | solution.py:148
  583.1 15.1 %conditional.14 = (bf16[4,128,320]{2,0,1:T(4,128)(2,1)S(1)}, bf16[2,64,640]{2,1,0:T(8,128)(2,1)}, bf16[2,64,640]{2,0,1:T(2,128)(2,1)}, bf16[1,40960]{1,0:T(2,128)(2,1)S(1)}, bf16[1,40960]{1,0:T(2,128)(2,1)S(1)}) conditional(s32[]{:T(128)} %clamp.14, (pred[]{:T(512)}, pred[]{:T(512)}, bf16[1,40960]{1,0:T(2,128)(2,1)S(1)}, ...), branch_computations={%region_29.29_spmd.clone, %region_30.30_spmd.clone, %region_31.31_... | conditional | flops 2017290240 | bytes 48206080 | solution.py:219
  603.8 3.0 collective-permute-done.5
  607.6 17.7 %all-reduce.5 = (f32[32]{0:T(128)S(1)}, f32[32]{0:T(128)S(1)}) all-reduce(f32[32]{0:T(128)S(1)} %get-tuple-element.971, f32[32]{0:T(128)S(1)} %get-tuple-element.972), channel_id=1, replica_groups=mesh['section'=4,'space'=8] {'space'}, use_global_device_ids=true, to_apply=%region_55.55 | all-reduce | flops 64 | bytes 512 | tf_op jit(solution)/shard_map/while/body/eval_jaxpr/psum | solution.py:148
  625.3 2.2 pad_maximum_fusion.6
  627.6 8.7 %conditional.16 = (bf16[4,128,320]{1,2,0:T(8,128)(2,1)S(1)}, bf16[2,64,640]{2,1,0:T(8,128)(2,1)S(1)}) conditional(s32[]{:T(128)} %clamp.14, (bf16[4,128,320]{2,0,1:T(4,128)(2,1)S(1)}, pred[]{:T(512)}, pred[]{:T(512)}, bf16[6,128,320]{2,1,0:T(8,128)(2,1)S(1)}, f32[32]{0:T(128)S(1)}, /*index=5*/f32[32]{0:T(128)S(1)}, ...), branch_computations={%region_57.57_spmd, %region_58.58_spmd, %region_59.59_spmd, %regio... | conditional | flops 1218529280 | bytes 43285440 | solution.py:262
  640.2 2.8 collective-permute-done.6
  644.6 122.9 %collective-permute-start.9 = (bf16[6,128,320]{1,2,0:T(8,128)(2,1)}, bf16[6,128,320]{1,2,0:T(8,128)(2,1)}, u32[]{:S(2)}, u32[]{:S(2)}) collective-permute-start(bf16[6,128,320]{1,2,0:T(8,128)(2,1)} %pad_maximum_fusion.7), channel_id=1, source_target_pairs={{0,24},{1,25},{2,26},{3,27},{4,28},{5,29},{6,30},{7,31}} | collective-permute-start | bytes 1474568 | tf_op jit(solution)/shard_map/while/body/eval_jaxpr/ppermute | solution.py:32
  771.1 3.4 collective-permute-done.9
  774.6 3.3 collective-permute-done.8
  779.2 1.9 copy.219
  781.1 29.3 %reduce-scatter.2.cloned.1.call-done = bf16[1,4,32,320]{3,2,1,0:T(8,128)(2,1)} async-done(((bf16[1,4,128,320]{3,2,1,0:T(8,128)(2,1)}), bf16[1,4,32,320]{3,2,1,0:T(8,128)(2,1)}) %reduce-scatter.2.cloned.1.call-update) | async-done | bytes 81936 | tf_op jit(solution)/shard_map/reduce_scatter | solution.py:306
  (376 shorter events, 108.5 us)
Async XLA Ops:
  6.5 86.6 %all-gather.2.cloned.1.call-start = ((), (), s32[]{:S(2)}) async-start(), calls=%async_computation.1 | async-start | bytes 16588800 | tf_op jit(solution)/shard_map/all_gather | solution.py:121
  7.3 803.1 %reduce-scatter.2.cloned.1.call-start = ((), (), s32[]{:S(2)}) async-start(), calls=%async_computation.2 | async-start | bytes 491520 | tf_op jit(solution)/shard_map/reduce_scatter | solution.py:306
  137.8 4.7 collective-permute-start.1
  139.1 4.0 collective-permute-start
  142.5 11.5 %copy-start = (bf16[4,128,320]{2,1,0:T(8,128)(2,1)}, bf16[4,128,320]{2,1,0:T(8,128)(2,1)S(1)}, u32[]{:S(2)}) copy-start(bf16[4,128,320]{2,1,0:T(8,128)(2,1)S(1)} %slice_bitcast_fusion.19) | copy-start | bytes 983044 | tf_op jit(solution)/shard_map/while
  150.6 19.1 %collective-permute-start.2 = (bf16[1,40960]{1,0:T(2,128)(2,1)S(1)}, bf16[1,40960]{1,0:T(2,128)(2,1)S(1)}, u32[]{:S(2)}, u32[]{:S(2)}) collective-permute-start(bf16[1,40960]{1,0:T(2,128)(2,1)S(1)} %get-tuple-element.955), channel_id=1, source_target_pairs={{0,1},{1,2},{2,3},{3,4},{4,5},{5,6},{6,7},{8,9},{9,10},{10,11},{11... | collective-permute-start | bytes 245768 | tf_op jit(solution)/shard_map/while/body/eval_jaxpr/ppermute | solution.py:23
  152.7 17.0 %collective-permute-start.3 = (bf16[1,40960]{1,0:T(2,128)(2,1)S(1)}, bf16[1,40960]{1,0:T(2,128)(2,1)S(1)}, u32[]{:S(2)}, u32[]{:S(2)}) collective-permute-start(bf16[1,40960]{1,0:T(2,128)(2,1)S(1)} %get-tuple-element.956), channel_id=1, source_target_pairs={{1,0},{2,1},{3,2},{4,3},{5,4},{6,5},{7,6},{9,8},{10,9},{11,10},{12... | collective-permute-start | bytes 245768 | tf_op jit(solution)/shard_map/while/body/eval_jaxpr/ppermute | solution.py:24
  169.7 0.7 copy-start.6
  170.5 2.1 copy-start.7
  170.5 2.6 copy-start.5
  177.5 0.7 copy-start.13
  199.9 2.6 collective-permute-start.4
  201.2 4.9 collective-permute-start.5
  206.7 20.4 %copy-start.1 = (bf16[4,128,320]{2,1,0:T(8,128)(2,1)S(1)}, bf16[4,128,320]{2,1,0:T(8,128)(2,1)}, u32[]{:S(2)}) copy-start(bf16[4,128,320]{2,1,0:T(8,128)(2,1)} %copy-done) | copy-start | bytes 983044 | tf_op jit(solution)/shard_map/while
  230.0 3.1 copy-start.16
  246.1 10.5 %copy-start.10 = (bf16[1,4,128,320]{2,3,1,0:T(8,128)(2,1)S(1)}, bf16[1,4,128,320]{2,3,1,0:T(8,128)(2,1)}, u32[]{:S(2)}) copy-start(bf16[1,4,128,320]{2,3,1,0:T(8,128)(2,1)} %get-tuple-element.1063) | copy-start | bytes 983044 | tf_op jit(solution)/shard_map/while
  246.4 2.9 collective-permute-start.7
  248.0 4.9 collective-permute-start.6
  254.5 20.6 %collective-permute-start.9 = (bf16[6,128,320]{1,2,0:T(8,128)(2,1)}, bf16[6,128,320]{1,2,0:T(8,128)(2,1)}, u32[]{:S(2)}, u32[]{:S(2)}) collective-permute-start(bf16[6,128,320]{1,2,0:T(8,128)(2,1)} %pad_maximum_fusion.7), channel_id=1, source_target_pairs={{0,24},{1,25},{2,26},{3,27},{4,28},{5,29},{6,30},{7,31}} | collective-permute-start | bytes 1474568 | tf_op jit(solution)/shard_map/while/body/eval_jaxpr/ppermute | solution.py:32
  256.6 0.7 copy-start.11
  269.7 0.7 copy-start.21
  273.8 4.1 collective-permute-start.8
  280.9 9.3 %collective-permute-start.1 = (bf16[1,40960]{1,0:T(2,128)(2,1)S(1)}, bf16[1,40960]{1,0:T(2,128)(2,1)S(1)}, u32[]{:S(2)}, u32[]{:S(2)}) collective-permute-start(bf16[1,40960]{1,0:T(2,128)(2,1)S(1)} %bitcast.271), channel_id=1, source_target_pairs={{1,0},{2,1},{3,2},{4,3},{5,4},{6,5},{7,6},{9,8},{10,9},{11,10},{12... | collective-permute-start | bytes 245768 | tf_op jit(solution)/shard_map/while/body/eval_jaxpr/ppermute | solution.py:24
  282.2 8.7 %collective-permute-start = (bf16[1,40960]{1,0:T(2,128)(2,1)S(1)}, bf16[1,40960]{1,0:T(2,128)(2,1)S(1)}, u32[]{:S(2)}, u32[]{:S(2)}) collective-permute-start(bf16[1,40960]{1,0:T(2,128)(2,1)S(1)} %bitcast.270), channel_id=1, source_target_pairs={{0,1},{1,2},{2,3},{3,4},{4,5},{5,6},{6,7},{8,9},{9,10},{10,11},{11... | collective-permute-start | bytes 245768 | tf_op jit(solution)/shard_map/while/body/eval_jaxpr/ppermute | solution.py:23
  290.3 11.7 %copy-start = (bf16[4,128,320]{2,1,0:T(8,128)(2,1)}, bf16[4,128,320]{2,1,0:T(8,128)(2,1)S(1)}, u32[]{:S(2)}) copy-start(bf16[4,128,320]{2,1,0:T(8,128)(2,1)S(1)} %slice_bitcast_fusion.19) | copy-start | bytes 983044 | tf_op jit(solution)/shard_map/while
  293.9 23.5 %collective-permute-start.2 = (bf16[1,40960]{1,0:T(2,128)(2,1)S(1)}, bf16[1,40960]{1,0:T(2,128)(2,1)S(1)}, u32[]{:S(2)}, u32[]{:S(2)}) collective-permute-start(bf16[1,40960]{1,0:T(2,128)(2,1)S(1)} %get-tuple-element.955), channel_id=1, source_target_pairs={{0,1},{1,2},{2,3},{3,4},{4,5},{5,6},{6,7},{8,9},{9,10},{10,11},{11... | collective-permute-start | bytes 245768 | tf_op jit(solution)/shard_map/while/body/eval_jaxpr/ppermute | solution.py:23
  300.6 16.8 %collective-permute-start.3 = (bf16[1,40960]{1,0:T(2,128)(2,1)S(1)}, bf16[1,40960]{1,0:T(2,128)(2,1)S(1)}, u32[]{:S(2)}, u32[]{:S(2)}) collective-permute-start(bf16[1,40960]{1,0:T(2,128)(2,1)S(1)} %get-tuple-element.956), channel_id=1, source_target_pairs={{1,0},{2,1},{3,2},{4,3},{5,4},{6,5},{7,6},{9,8},{10,9},{11,10},{12... | collective-permute-start | bytes 245768 | tf_op jit(solution)/shard_map/while/body/eval_jaxpr/ppermute | solution.py:24
  334.8 3.1 collective-permute-start.4
  336.7 5.1 collective-permute-start.5
  342.3 20.2 %copy-start.1 = (bf16[4,128,320]{2,1,0:T(8,128)(2,1)S(1)}, bf16[4,128,320]{2,1,0:T(8,128)(2,1)}, u32[]{:S(2)}) copy-start(bf16[4,128,320]{2,1,0:T(8,128)(2,1)} %copy-done) | copy-start | bytes 983044 | tf_op jit(solution)/shard_map/while
  371.2 10.5 %copy-start.10 = (bf16[1,4,128,320]{2,3,1,0:T(8,128)(2,1)S(1)}, bf16[1,4,128,320]{2,3,1,0:T(8,128)(2,1)}, u32[]{:S(2)}) copy-start(bf16[1,4,128,320]{2,3,1,0:T(8,128)(2,1)} %get-tuple-element.1063) | copy-start | bytes 983044 | tf_op jit(solution)/shard_map/while
  371.5 2.9 collective-permute-start.7
  373.1 4.9 collective-permute-start.6
  379.6 52.0 %collective-permute-start.9 = (bf16[6,128,320]{1,2,0:T(8,128)(2,1)}, bf16[6,128,320]{1,2,0:T(8,128)(2,1)}, u32[]{:S(2)}, u32[]{:S(2)}) collective-permute-start(bf16[6,128,320]{1,2,0:T(8,128)(2,1)} %pad_maximum_fusion.7), channel_id=1, source_target_pairs={{0,24},{1,25},{2,26},{3,27},{4,28},{5,29},{6,30},{7,31}} | collective-permute-start | bytes 1474568 | tf_op jit(solution)/shard_map/while/body/eval_jaxpr/ppermute | solution.py:32
  381.7 0.7 copy-start.11
  384.0 50.5 %collective-permute-start.8 = (bf16[2,64,640]{2,0,1:T(2,128)(2,1)S(1)}, bf16[2,64,640]{2,0,1:T(2,128)(2,1)S(1)}, u32[]{:S(2)}, u32[]{:S(2)}) collective-permute-start(bf16[2,64,640]{2,0,1:T(2,128)(2,1)S(1)} %get-tuple-element.1090), channel_id=1, source_target_pairs={{0,8},{8,16},{16,24},{1,9},{9,17},{17,25},{2,10},{10,18},{18,26},{... | collective-permute-start | bytes 491528 | tf_op jit(solution)/shard_map/while/body/eval_jaxpr/ppermute | solution.py:32
  434.9 8.5 %collective-permute-start.1 = (bf16[1,40960]{1,0:T(2,128)(2,1)S(1)}, bf16[1,40960]{1,0:T(2,128)(2,1)S(1)}, u32[]{:S(2)}, u32[]{:S(2)}) collective-permute-start(bf16[1,40960]{1,0:T(2,128)(2,1)S(1)} %bitcast.271), channel_id=1, source_target_pairs={{1,0},{2,1},{3,2},{4,3},{5,4},{6,5},{7,6},{9,8},{10,9},{11,10},{12... | collective-permute-start | bytes 245768 | tf_op jit(solution)/shard_map/while/body/eval_jaxpr/ppermute | solution.py:24
  436.2 7.8 collective-permute-start
  443.4 11.7 %copy-start = (bf16[4,128,320]{2,1,0:T(8,128)(2,1)}, bf16[4,128,320]{2,1,0:T(8,128)(2,1)S(1)}, u32[]{:S(2)}) copy-start(bf16[4,128,320]{2,1,0:T(8,128)(2,1)S(1)} %slice_bitcast_fusion.19) | copy-start | bytes 983044 | tf_op jit(solution)/shard_map/while
  447.6 23.2 %collective-permute-start.2 = (bf16[1,40960]{1,0:T(2,128)(2,1)S(1)}, bf16[1,40960]{1,0:T(2,128)(2,1)S(1)}, u32[]{:S(2)}, u32[]{:S(2)}) collective-permute-start(bf16[1,40960]{1,0:T(2,128)(2,1)S(1)} %get-tuple-element.955), channel_id=1, source_target_pairs={{0,1},{1,2},{2,3},{3,4},{4,5},{5,6},{6,7},{8,9},{9,10},{10,11},{11... | collective-permute-start | bytes 245768 | tf_op jit(solution)/shard_map/while/body/eval_jaxpr/ppermute | solution.py:23
  453.7 17.0 %collective-permute-start.3 = (bf16[1,40960]{1,0:T(2,128)(2,1)S(1)}, bf16[1,40960]{1,0:T(2,128)(2,1)S(1)}, u32[]{:S(2)}, u32[]{:S(2)}) collective-permute-start(bf16[1,40960]{1,0:T(2,128)(2,1)S(1)} %get-tuple-element.956), channel_id=1, source_target_pairs={{1,0},{2,1},{3,2},{4,3},{5,4},{6,5},{7,6},{9,8},{10,9},{11,10},{12... | collective-permute-start | bytes 245768 | tf_op jit(solution)/shard_map/while/body/eval_jaxpr/ppermute | solution.py:24
  488.2 2.9 collective-permute-start.4
  489.8 5.1 collective-permute-start.5
  495.4 20.2 %copy-start.1 = (bf16[4,128,320]{2,1,0:T(8,128)(2,1)S(1)}, bf16[4,128,320]{2,1,0:T(8,128)(2,1)}, u32[]{:S(2)}) copy-start(bf16[4,128,320]{2,1,0:T(8,128)(2,1)} %copy-done) | copy-start | bytes 983044 | tf_op jit(solution)/shard_map/while
  524.3 10.5 %copy-start.10 = (bf16[1,4,128,320]{2,3,1,0:T(8,128)(2,1)S(1)}, bf16[1,4,128,320]{2,3,1,0:T(8,128)(2,1)}, u32[]{:S(2)}) copy-start(bf16[1,4,128,320]{2,3,1,0:T(8,128)(2,1)} %get-tuple-element.1063) | copy-start | bytes 983044 | tf_op jit(solution)/shard_map/while
  524.7 2.9 collective-permute-start.7
  526.3 4.9 collective-permute-start.6
  532.7 8.8 %collective-permute-start.9 = (bf16[6,128,320]{1,2,0:T(8,128)(2,1)}, bf16[6,128,320]{1,2,0:T(8,128)(2,1)}, u32[]{:S(2)}, u32[]{:S(2)}) collective-permute-start(bf16[6,128,320]{1,2,0:T(8,128)(2,1)} %pad_maximum_fusion.7), channel_id=1, source_target_pairs={{0,24},{1,25},{2,26},{3,27},{4,28},{5,29},{6,30},{7,31}} | collective-permute-start | bytes 1474568 | tf_op jit(solution)/shard_map/while/body/eval_jaxpr/ppermute | solution.py:32
  534.9 0.7 copy-start.11
  537.1 8.7 %collective-permute-start.8 = (bf16[2,64,640]{2,0,1:T(2,128)(2,1)S(1)}, bf16[2,64,640]{2,0,1:T(2,128)(2,1)S(1)}, u32[]{:S(2)}, u32[]{:S(2)}) collective-permute-start(bf16[2,64,640]{2,0,1:T(2,128)(2,1)S(1)} %get-tuple-element.1090), channel_id=1, source_target_pairs={{0,8},{8,16},{16,24},{1,9},{9,17},{17,25},{2,10},{10,18},{18,26},{... | collective-permute-start | bytes 491528 | tf_op jit(solution)/shard_map/while/body/eval_jaxpr/ppermute | solution.py:32
  546.2 7.9 collective-permute-start.1
  547.5 7.3 collective-permute-start
  554.1 11.7 %copy-start = (bf16[4,128,320]{2,1,0:T(8,128)(2,1)}, bf16[4,128,320]{2,1,0:T(8,128)(2,1)S(1)}, u32[]{:S(2)}) copy-start(bf16[4,128,320]{2,1,0:T(8,128)(2,1)S(1)} %slice_bitcast_fusion.19) | copy-start | bytes 983044 | tf_op jit(solution)/shard_map/while
  558.9 24.2 %collective-permute-start.2 = (bf16[1,40960]{1,0:T(2,128)(2,1)S(1)}, bf16[1,40960]{1,0:T(2,128)(2,1)S(1)}, u32[]{:S(2)}, u32[]{:S(2)}) collective-permute-start(bf16[1,40960]{1,0:T(2,128)(2,1)S(1)} %get-tuple-element.955), channel_id=1, source_target_pairs={{0,1},{1,2},{2,3},{3,4},{4,5},{5,6},{6,7},{8,9},{9,10},{10,11},{11... | collective-permute-start | bytes 245768 | tf_op jit(solution)/shard_map/while/body/eval_jaxpr/ppermute | solution.py:23
  564.5 18.6 %collective-permute-start.3 = (bf16[1,40960]{1,0:T(2,128)(2,1)S(1)}, bf16[1,40960]{1,0:T(2,128)(2,1)S(1)}, u32[]{:S(2)}, u32[]{:S(2)}) collective-permute-start(bf16[1,40960]{1,0:T(2,128)(2,1)S(1)} %get-tuple-element.956), channel_id=1, source_target_pairs={{1,0},{2,1},{3,2},{4,3},{5,4},{6,5},{7,6},{9,8},{10,9},{11,10},{12... | collective-permute-start | bytes 245768 | tf_op jit(solution)/shard_map/while/body/eval_jaxpr/ppermute | solution.py:24
  600.5 2.6 collective-permute-start.4
  601.8 4.9 collective-permute-start.5
  607.4 20.2 %copy-start.1 = (bf16[4,128,320]{2,1,0:T(8,128)(2,1)S(1)}, bf16[4,128,320]{2,1,0:T(8,128)(2,1)}, u32[]{:S(2)}) copy-start(bf16[4,128,320]{2,1,0:T(8,128)(2,1)} %copy-done) | copy-start | bytes 983044 | tf_op jit(solution)/shard_map/while
  636.2 131.3 %copy-start.10 = (bf16[1,4,128,320]{2,3,1,0:T(8,128)(2,1)S(1)}, bf16[1,4,128,320]{2,3,1,0:T(8,128)(2,1)}, u32[]{:S(2)}) copy-start(bf16[1,4,128,320]{2,3,1,0:T(8,128)(2,1)} %get-tuple-element.1063) | copy-start | bytes 983044 | tf_op jit(solution)/shard_map/while
  636.6 2.9 collective-permute-start.7
  638.2 4.9 collective-permute-start.6
  644.6 129.9 %collective-permute-start.9 = (bf16[6,128,320]{1,2,0:T(8,128)(2,1)}, bf16[6,128,320]{1,2,0:T(8,128)(2,1)}, u32[]{:S(2)}, u32[]{:S(2)}) collective-permute-start(bf16[6,128,320]{1,2,0:T(8,128)(2,1)} %pad_maximum_fusion.7), channel_id=1, source_target_pairs={{0,24},{1,25},{2,26},{3,27},{4,28},{5,29},{6,30},{7,31}} | collective-permute-start | bytes 1474568 | tf_op jit(solution)/shard_map/while/body/eval_jaxpr/ppermute | solution.py:32
  767.6 0.7 copy-start.11
  769.8 8.1 collective-permute-start.8
  (1 other events, 0.7 us)
Sparse Core Ops, SparseCore 0:
  9.2 83.8 all-gather.1
  781.2 29.1 reduce-scatter.1
where the time goes:
time: 823 us; the launch traced here: 818 us
  starting transfers between devices  260 us (32%)
  waiting for transfers between devices  158 us (19%)
  blocking collectives  134 us (16%)
  local copies, waits for them, and re-layouts  106 us (13%)
  loops' own time  106 us (13%)
  other arithmetic  29.3 us (4%)
  between operations  13.7 us (2%)
  matrix products  9.8 us (1%)
    ppermute x8, starting transfers between devices, passed_along(): lax.ppermute(value, axis, [(source, source + steps) for source in range(i...  183 us
    psum x8, blocking collectives, moments(): group_mean, mean_square = lax.psum((first_part, second_part), 'space')  134 us
    all_gather x1, waiting for transfers between devices, shards(): gathered = lax.all_gather(section_packs, 'space', axis=2, tiled=True)  85.8 us
    ppermute x16, starting transfers between devices, padded(): before = lax.ppermute(last, axis, up)  55.5 us
    another operation x4, loops' own time, section_tick(): hidden_fine, hidden_coarse = lax.switch(branch_pick, branches(first_conv))  54.2 us
    another operation x4, loops' own time, section_tick(): out_fine, out_coarse = lax.switch(branch_pick, branches(second_conv))  34.7 us
    reduce_scatter x1, waiting for transfers between devices, shards(): lax.psum_scatter(results.astype(jnp.float32).astype(jnp.bfloat16), 'secti...  29.3 us
    reshape x1, local copies, waits for them, and re-layouts, shards(): flat_pack = gathered.reshape(-1)  24.4 us
  transfers between devices with their start and end apart: 42, of which 20 were waited for; matrix products, arithmetic and copies ran while one was open for 3% of the time, Pallas kernels for 0%

commit v1 on v0

--- a/solution.py
+++ b/solution.py
@@ -7,6 +7,19 @@
 
 GROUPS = 32
 EPSILON = 1e-05
+
+
+def gather_around(array, axis, dim):
+    peers, place, rows = (lax.axis_size(axis), lax.axis_index(axis), array.shape[dim])
+    ahead = [(i, (i + 1) % peers) for i in range(peers)]
+    filled = jnp.zeros((*array.shape[:dim], peers * rows, *array.shape[dim + 1 :]), array.dtype)
+    current = array
+    for lap in range(peers):
+        source = (place - lap) % peers
+        filled = lax.dynamic_update_slice_in_dim(filled, current, source * rows, axis=dim)
+        if lap < peers - 1:
+            current = lax.ppermute(current, axis, ahead)
+    return filled
 
 
 def for_sending(x):
@@ -118,7 +131,7 @@
     fine_zero = jnp.zeros(fine_shape, jnp.bfloat16)
     coarse_zero = jnp.zeros(coarse_shape, jnp.bfloat16)
     is_fine = (section_id == 0) | (section_id == 3)
-    gathered = lax.all_gather(section_packs, "space", axis=2, tiled=True)
+    gathered = gather_around(section_packs, "space", 2)
     flat_pack = gathered.reshape(-1)
     ghost_rows = 1
 

time: 823 us -> 1140 us (1.39); the launches traced: 818 us -> 1120 us
  local copies, waits for them, and re-layouts: 106 us -> 377 us
  waiting for transfers between devices: 158 us -> 219 us
    dynamic_update_slice x0 -> x8, local copies, waits for them, and re-layouts: none -> 246 us  [gather_around(): lax.dynamic_update_slice_in_dim(filled, current, source * rows, axis=dim)]
    ppermute x0 -> x7, waiting for transfers between devices: none -> 142 us  [gather_around(): current = lax.ppermute(current, axis, ahead)]
    all_gather x1 -> x0, waiting for transfers between devices: 85.8 us -> none  [shards(): gathered = lax.all_gather(section_packs, 'space', axis=2, tiled=True)]
    ppermute x0 -> x7, local copies, waits for them, and re-layouts: none -> 27.6 us  [gather_around(): current = lax.ppermute(current, axis, ahead)]
    all_gather x1 -> x0, local copies, waits for them, and re-layouts: 18.7 us -> none  [shards(): gathered = lax.all_gather(section_packs, 'space', axis=2, tiled=True)]
  transfers between devices with their start and end apart: 42 -> 48, of which waited for: 20 -> 25; matrix products, arithmetic and copies ran while one was open for 3% -> 24% of each run, Pallas kernels for 0% -> 0%
where the time goes in v1:
time: 1140 us; the launch traced here: 1120 us
  local copies, waits for them, and re-layouts  377 us (33%)
  starting transfers between devices  249 us (22%)
  waiting for transfers between devices  219 us (19%)
  blocking collectives  126 us (11%)
  loops' own time  102 us (9%)
  other arithmetic  26.2 us (2%)
  between operations  13.9 us (1%)
    dynamic_update_slice x8, local copies, waits for them, and re-layouts, gather_around(): lax.dynamic_update_slice_in_dim(filled, current, source * rows, axis=dim)  246 us
    ppermute x8, starting transfers between devices, passed_along(): lax.ppermute(value, axis, [(source, source + steps) for source in range(i...  174 us
    ppermute x7, waiting for transfers between devices, gather_around(): current = lax.ppermute(current, axis, ahead)  142 us
    psum x8, blocking collectives, moments(): group_mean, mean_square = lax.psum((first_part, second_part), 'space')  126 us
    ppermute x16, starting transfers between devices, padded(): before = lax.ppermute(last, axis, up)  53.4 us
    another operation x4, loops' own time, section_tick(): hidden_fine, hidden_coarse = lax.switch(branch_pick, branches(first_conv))  51.3 us
    another operation x4, loops' own time, section_tick(): out_fine, out_coarse = lax.switch(branch_pick, branches(second_conv))  34.2 us
    ppermute x7, local copies, waits for them, and re-layouts, gather_around(): current = lax.ppermute(current, axis, ahead)  27.6 us
  transfers between devices with their start and end apart: 48, of which 25 were waited for; matrix products, arithmetic and copies ran while one was open for 24% of the time, Pallas kernels for 0%

profile of v1, /device:TPU:0, one launch (start us, length us, event | category | flops | bytes accessed | tf_op | source)
XLA Modules:
  0.0 1122.9 jit_solution(11714566228729851973)
XLA Ops:
  7.0 24.1 %collective-permute-done.10 = bf16[1,11520,80]{1,2,0:T(8,128)(2,1)S(1)} collective-permute-done((bf16[1,11520,80]{1,2,0:T(8,128)(2,1)}, bf16[1,11520,80]{1,2,0:T(8,128)(2,1)S(1)}, u32[]{:S(2)}, u32[]{:S(2)}) %collective-permute-start.10) | collective-permute-done | bytes 1843232 | tf_op jit(solution)/shard_map/ppermute | solution.py:21
  32.4 23.6 %collective-permute-done.11 = bf16[1,11520,80]{1,2,0:T(8,128)(2,1)S(1)} collective-permute-done((bf16[1,11520,80]{1,2,0:T(8,128)(2,1)S(1)}, bf16[1,11520,80]{1,2,0:T(8,128)(2,1)S(1)}, u32[]{:S(2)}, u32[]{:S(2)}) %collective-permute-start.11) | collective-permute-done | bytes 1843232 | tf_op jit(solution)/shard_map/ppermute | solution.py:21
  57.2 23.6 %collective-permute-done.12 = bf16[1,11520,80]{1,2,0:T(8,128)(2,1)S(1)} collective-permute-done((bf16[1,11520,80]{1,2,0:T(8,128)(2,1)S(1)}, bf16[1,11520,80]{1,2,0:T(8,128)(2,1)S(1)}, u32[]{:S(2)}, u32[]{:S(2)}) %collective-permute-start.12) | collective-permute-done | bytes 1843232 | tf_op jit(solution)/shard_map/ppermute | solution.py:21
  82.2 23.6 %collective-permute-done.13 = bf16[1,11520,80]{1,2,0:T(8,128)(2,1)S(1)} collective-permute-done((bf16[1,11520,80]{1,2,0:T(8,128)(2,1)S(1)}, bf16[1,11520,80]{1,2,0:T(8,128)(2,1)S(1)}, u32[]{:S(2)}, u32[]{:S(2)}) %collective-permute-start.13) | collective-permute-done | bytes 1843232 | tf_op jit(solution)/shard_map/ppermute | solution.py:21
  107.1 23.6 %collective-permute-done.14 = bf16[1,11520,80]{1,2,0:T(8,128)(2,1)S(1)} collective-permute-done((bf16[1,11520,80]{1,2,0:T(8,128)(2,1)S(1)}, bf16[1,11520,80]{1,2,0:T(8,128)(2,1)S(1)}, u32[]{:S(2)}, u32[]{:S(2)}) %collective-permute-start.14) | collective-permute-done | bytes 1843232 | tf_op jit(solution)/shard_map/ppermute | solution.py:21
  132.0 23.7 %collective-permute-done.15 = bf16[1,11520,80]{1,2,0:T(8,128)(2,1)} collective-permute-done((bf16[1,11520,80]{1,2,0:T(8,128)(2,1)S(1)}, bf16[1,11520,80]{1,2,0:T(8,128)(2,1)}, u32[]{:S(2)}, u32[]{:S(2)}) %collective-permute-start.15) | collective-permute-done | bytes 1843232 | tf_op jit(solution)/shard_map/ppermute | solution.py:21
  155.7 3.9 copy.232
  159.8 5.4 broadcast_in_dim.149
  165.2 27.3 %dynamic_update_slice.32 = bf16[1,11520,640]{2,1,0:T(8,128)(2,1)} dynamic-update-slice(bf16[1,11520,640]{2,1,0:T(8,128)(2,1)} %broadcast_in_dim.149, bf16[1,11520,80]{2,1,0:T(8,128)(2,1)S(1)} %copy.232, s32[]{:T(128)} %constant.302.clone.1, s32[]{:T(128)} %constant.302.clone.1, s32[]{:T(128)S(6)} %select_n.202) | dynamic-update-slice | bytes 3686404 | tf_op jit(solution)/shard_map/dynamic_update_slice | solution.py:19
  192.5 3.9 copy.233
  196.4 30.5 %dynamic_update_slice.33 = bf16[1,11520,640]{2,1,0:T(8,128)(2,1)} dynamic-update-slice(bf16[1,11520,640]{2,1,0:T(8,128)(2,1)} %dynamic_update_slice.32, bf16[1,11520,80]{2,1,0:T(8,128)(2,1)S(1)} %copy.233, s32[]{:T(128)} %constant.302.clone.1, s32[]{:T(128)} %constant.302.clone.1, s32[]{:T(128)S(6)} %select_n.204) | dynamic-update-slice | bytes 3686404 | tf_op jit(solution)/shard_map/dynamic_update_slice | solution.py:19
  226.9 3.9 copy.234
  230.8 31.4 %dynamic_update_slice.34 = bf16[1,11520,640]{2,1,0:T(8,128)(2,1)} dynamic-update-slice(bf16[1,11520,640]{2,1,0:T(8,128)(2,1)} %dynamic_update_slice.33, bf16[1,11520,80]{2,1,0:T(8,128)(2,1)S(1)} %copy.234, s32[]{:T(128)} %constant.302.clone.1, s32[]{:T(128)} %constant.302.clone.1, s32[]{:T(128)S(6)} %select_n.206) | dynamic-update-slice | bytes 3686404 | tf_op jit(solution)/shard_map/dynamic_update_slice | solution.py:19
  262.3 3.9 copy.235
  266.2 31.4 %dynamic_update_slice.35 = bf16[1,11520,640]{2,1,0:T(8,128)(2,1)} dynamic-update-slice(bf16[1,11520,640]{2,1,0:T(8,128)(2,1)} %dynamic_update_slice.34, bf16[1,11520,80]{2,1,0:T(8,128)(2,1)S(1)} %copy.235, s32[]{:T(128)} %constant.302.clone.1, s32[]{:T(128)} %constant.302.clone.1, s32[]{:T(128)S(6)} %select_n.208) | dynamic-update-slice | bytes 3686404 | tf_op jit(solution)/shard_map/dynamic_update_slice | solution.py:19
  297.7 3.9 copy.236
  301.6 31.4 %dynamic_update_slice.36 = bf16[1,11520,640]{2,1,0:T(8,128)(2,1)} dynamic-update-slice(bf16[1,11520,640]{2,1,0:T(8,128)(2,1)} %dynamic_update_slice.35, bf16[1,11520,80]{2,1,0:T(8,128)(2,1)S(1)} %copy.236, s32[]{:T(128)} %constant.302.clone.1, s32[]{:T(128)} %constant.302.clone.1, s32[]{:T(128)S(6)} %select_n.210) | dynamic-update-slice | bytes 3686404 | tf_op jit(solution)/shard_map/dynamic_update_slice | solution.py:19
  333.0 3.9 copy.237
  337.0 31.4 %dynamic_update_slice.37 = bf16[1,11520,640]{2,1,0:T(8,128)(2,1)} dynamic-update-slice(bf16[1,11520,640]{2,1,0:T(8,128)(2,1)} %dynamic_update_slice.36, bf16[1,11520,80]{2,1,0:T(8,128)(2,1)S(1)} %copy.237, s32[]{:T(128)} %constant.302.clone.1, s32[]{:T(128)} %constant.302.clone.1, s32[]{:T(128)S(6)} %select_n.212) | dynamic-update-slice | bytes 3686404 | tf_op jit(solution)/shard_map/dynamic_update_slice | solution.py:19
  368.4 3.9 copy.238
  372.4 31.4 %dynamic_update_slice.38 = bf16[1,11520,640]{2,1,0:T(8,128)(2,1)} dynamic-update-slice(bf16[1,11520,640]{2,1,0:T(8,128)(2,1)} %dynamic_update_slice.37, bf16[1,11520,80]{2,1,0:T(8,128)(2,1)S(1)} %copy.238, s32[]{:T(128)} %constant.302.clone.1, s32[]{:T(128)} %constant.302.clone.1, s32[]{:T(128)S(6)} %select_n.214) | dynamic-update-slice | bytes 3686404 | tf_op jit(solution)/shard_map/dynamic_update_slice | solution.py:19
  403.8 3.9 copy.239
  407.7 31.4 %dynamic_update_slice.39 = bf16[1,11520,640]{2,1,0:T(8,128)(2,1)} dynamic-update-slice(bf16[1,11520,640]{2,1,0:T(8,128)(2,1)} %dynamic_update_slice.38, bf16[1,11520,80]{2,1,0:T(8,128)(2,1)S(1)} %copy.239, s32[]{:T(128)} %constant.302.clone.1, s32[]{:T(128)} %constant.302.clone.1, s32[]{:T(128)S(6)} %select_n.216) | dynamic-update-slice | bytes 3686404 | tf_op jit(solution)/shard_map/dynamic_update_slice | solution.py:19
  439.2 24.4 %reshape.795 = bf16[7372800]{0:T(1024)(128)(2,1)} reshape(bf16[1,11520,640]{2,1,0:T(8,128)(2,1)} %dynamic_update_slice.39) | data formatting | bytes 29491200 | tf_op jit(solution)/shard_map/reshape | solution.py:135
  464.6 623.3 %while.24 = (s32[]{:T(128)}, bf16[2,64,640]{2,0,1:T(2,128)(2,1)S(1)}, bf16[1,6,128,320]{2,3,1,0:T(8,128)(2,1)S(1)}, bf16[1,4,128,320]{2,3,1,0:T(8,128)(2,1)}, s3...) while((s32[]{:T(128)}, ...), condition=%wide.region_67.68_spmd, body=%wide.region_0.67_spmd.sunk | while | flops 5784842240 | bytes 182410480 | solution.py:315
  470.5 4.7 conditional.12
  477.9 4.2 collective-permute-start.2
  484.0 13.2 %all-reduce.4 = (f32[32]{0:T(128)S(1)}, f32[32]{0:T(128)S(1)}) all-reduce(f32[32]{0:T(128)S(1)} %get-tuple-element.957, f32[32]{0:T(128)S(1)} %get-tuple-element.958), channel_id=1, replica_groups=mesh['section'=4,'space'=8] {'space'}, use_global_device_ids=true, to_apply=%region_27.27 | all-reduce | flops 64 | bytes 512 | tf_op jit(solution)/shard_map/while/body/eval_jaxpr/psum | solution.py:161
  497.3 26.9 %conditional.14 = (bf16[4,128,320]{2,0,1:T(4,128)(2,1)S(1)}, bf16[2,64,640]{2,1,0:T(8,128)(2,1)}, bf16[2,64,640]{2,0,1:T(2,128)(2,1)}, bf16[1,40960]{1,0:T(2,128)(2,1)S(1)}, bf16[1,40960]{1,0:T(2,128)(2,1)S(1)}) conditional(s32[]{:T(128)} %clamp.14, (pred[]{:T(512)}, pred[]{:T(512)}, bf16[1,40960]{1,0:T(2,128)(2,1)S(1)}, ...), branch_computations={%region_29.29_spmd.clone, %region_30.30_spmd.clone, %region_31.31_... | conditional | flops 2017290240 | bytes 56561976 | solution.py:232
  505.4 3.7 fusion.129
  533.3 17.7 %all-reduce.5 = (f32[32]{0:T(128)S(1)}, f32[32]{0:T(128)S(1)}) all-reduce(f32[32]{0:T(128)S(1)} %get-tuple-element.971, f32[32]{0:T(128)S(1)} %get-tuple-element.972), channel_id=1, replica_groups=mesh['section'=4,'space'=8] {'space'}, use_global_device_ids=true, to_apply=%region_55.55 | all-reduce | flops 64 | bytes 512 | tf_op jit(solution)/shard_map/while/body/eval_jaxpr/psum | solution.py:161
  552.5 18.8 %conditional.16 = (bf16[4,128,320]{1,2,0:T(8,128)(2,1)S(1)}, bf16[2,64,640]{2,1,0:T(8,128)(2,1)S(1)}) conditional(s32[]{:T(128)} %clamp.14, (bf16[4,128,320]{2,0,1:T(4,128)(2,1)S(1)}, pred[]{:T(512)}, pred[]{:T(512)}, bf16[6,128,320]{2,1,0:T(8,128)(2,1)S(1)}, f32[32]{0:T(128)S(1)}, /*index=5*/f32[32]{0:T(128)S(1)}, ...), branch_computations={%region_57.57_spmd, %region_58.58_spmd, %region_59.59_spmd, %regio... | conditional | flops 1218529280 | bytes 41974688 | solution.py:275
  558.6 3.5 fusion.9
  581.0 16.5 %conditional.17 = (bf16[2,64,640]{2,0,1:T(2,128)(2,1)S(1)}) conditional(s32[]{:T(128)} %clamp.14, (bf16[6,128,320]{1,2,0:T(8,128)(2,1)}, bf16[7372800]{0:T(1024)(128)(2,1)}) %tuple.329, bf16[2,64,640]{2,1,0:T(8,128)(2,1)S(1)} %get-tuple-element.979, bf16[2,64,640]{2,1,0:T(8,128)(2,1)S(1)} %get-tuple-element.979, ...), branch_computations={%region_62.62_spmd, %region_63.63_spmd, %region_64.64_spmd, %regio... | conditional | flops 532961280 | bytes 24266638 | solution.py:292
  583.2 3.4 slice.261
  586.6 7.2 slice.262
  604.6 4.1 collective-permute-start
  610.5 3.6 collective-permute-done.1
  617.2 6.6 collective-permute-start.2
  625.2 14.8 %all-reduce.4 = (f32[32]{0:T(128)S(1)}, f32[32]{0:T(128)S(1)}) all-reduce(f32[32]{0:T(128)S(1)} %get-tuple-element.957, f32[32]{0:T(128)S(1)} %get-tuple-element.958), channel_id=1, replica_groups=mesh['section'=4,'space'=8] {'space'}, use_global_device_ids=true, to_apply=%region_27.27 | all-reduce | flops 64 | bytes 512 | tf_op jit(solution)/shard_map/while/body/eval_jaxpr/psum | solution.py:161
  640.0 14.4 %conditional.14 = (bf16[4,128,320]{2,0,1:T(4,128)(2,1)S(1)}, bf16[2,64,640]{2,1,0:T(8,128)(2,1)}, bf16[2,64,640]{2,0,1:T(2,128)(2,1)}, bf16[1,40960]{1,0:T(2,128)(2,1)S(1)}, bf16[1,40960]{1,0:T(2,128)(2,1)S(1)}) conditional(s32[]{:T(128)} %clamp.14, (pred[]{:T(512)}, pred[]{:T(512)}, bf16[1,40960]{1,0:T(2,128)(2,1)S(1)}, ...), branch_computations={%region_29.29_spmd.clone, %region_30.30_spmd.clone, %region_31.31_... | conditional | flops 2017290240 | bytes 56561976 | solution.py:232
  663.7 17.7 %all-reduce.5 = (f32[32]{0:T(128)S(1)}, f32[32]{0:T(128)S(1)}) all-reduce(f32[32]{0:T(128)S(1)} %get-tuple-element.971, f32[32]{0:T(128)S(1)} %get-tuple-element.972), channel_id=1, replica_groups=mesh['section'=4,'space'=8] {'space'}, use_global_device_ids=true, to_apply=%region_55.55 | all-reduce | flops 64 | bytes 512 | tf_op jit(solution)/shard_map/while/body/eval_jaxpr/psum | solution.py:161
  682.9 8.7 conditional.16
  702.8 49.0 %collective-permute-start.8 = (bf16[2,64,640]{2,0,1:T(2,128)(2,1)S(1)}, bf16[2,64,640]{2,0,1:T(2,128)(2,1)S(1)}, u32[]{:S(2)}, u32[]{:S(2)}) collective-permute-start(bf16[2,64,640]{2,0,1:T(2,128)(2,1)S(1)} %get-tuple-element.1090), channel_id=1, source_target_pairs={{0,8},{8,16},{16,24},{1,9},{9,17},{17,25},{2,10},{10,18},{18,26},{... | collective-permute-start | bytes 491528 | tf_op jit(solution)/shard_map/while/body/eval_jaxpr/ppermute | solution.py:45
  760.6 5.0 collective-permute-done.1
  768.8 7.1 collective-permute-start.2
  777.3 13.4 %all-reduce.4 = (f32[32]{0:T(128)S(1)}, f32[32]{0:T(128)S(1)}) all-reduce(f32[32]{0:T(128)S(1)} %get-tuple-element.957, f32[32]{0:T(128)S(1)} %get-tuple-element.958), channel_id=1, replica_groups=mesh['section'=4,'space'=8] {'space'}, use_global_device_ids=true, to_apply=%region_27.27 | all-reduce | flops 64 | bytes 512 | tf_op jit(solution)/shard_map/while/body/eval_jaxpr/psum | solution.py:161
  790.7 14.3 %conditional.14 = (bf16[4,128,320]{2,0,1:T(4,128)(2,1)S(1)}, bf16[2,64,640]{2,1,0:T(8,128)(2,1)}, bf16[2,64,640]{2,0,1:T(2,128)(2,1)}, bf16[1,40960]{1,0:T(2,128)(2,1)S(1)}, bf16[1,40960]{1,0:T(2,128)(2,1)S(1)}) conditional(s32[]{:T(128)} %clamp.14, (pred[]{:T(512)}, pred[]{:T(512)}, bf16[1,40960]{1,0:T(2,128)(2,1)S(1)}, ...), branch_computations={%region_29.29_spmd.clone, %region_30.30_spmd.clone, %region_31.31_... | conditional | flops 2017290240 | bytes 56561976 | solution.py:232
  814.3 17.7 %all-reduce.5 = (f32[32]{0:T(128)S(1)}, f32[32]{0:T(128)S(1)}) all-reduce(f32[32]{0:T(128)S(1)} %get-tuple-element.971, f32[32]{0:T(128)S(1)} %get-tuple-element.972), channel_id=1, replica_groups=mesh['section'=4,'space'=8] {'space'}, use_global_device_ids=true, to_apply=%region_55.55 | all-reduce | flops 64 | bytes 512 | tf_op jit(solution)/shard_map/while/body/eval_jaxpr/psum | solution.py:161
  833.5 8.7 conditional.16
  853.4 3.7 collective-permute-start.8
  857.1 4.2 collective-permute-done.9
  861.4 3.3 collective-permute-done.8
  865.4 3.6 collective-permute-start
  870.7 4.7 collective-permute-done.1
  878.3 5.8 collective-permute-start.2
  885.5 13.5 %all-reduce.4 = (f32[32]{0:T(128)S(1)}, f32[32]{0:T(128)S(1)}) all-reduce(f32[32]{0:T(128)S(1)} %get-tuple-element.957, f32[32]{0:T(128)S(1)} %get-tuple-element.958), channel_id=1, replica_groups=mesh['section'=4,'space'=8] {'space'}, use_global_device_ids=true, to_apply=%region_27.27 | all-reduce | flops 64 | bytes 512 | tf_op jit(solution)/shard_map/while/body/eval_jaxpr/psum | solution.py:161
  898.9 14.4 %conditional.14 = (bf16[4,128,320]{2,0,1:T(4,128)(2,1)S(1)}, bf16[2,64,640]{2,1,0:T(8,128)(2,1)}, bf16[2,64,640]{2,0,1:T(2,128)(2,1)}, bf16[1,40960]{1,0:T(2,128)(2,1)S(1)}, bf16[1,40960]{1,0:T(2,128)(2,1)S(1)}) conditional(s32[]{:T(128)} %clamp.14, (pred[]{:T(512)}, pred[]{:T(512)}, bf16[1,40960]{1,0:T(2,128)(2,1)S(1)}, ...), branch_computations={%region_29.29_spmd.clone, %region_30.30_spmd.clone, %region_31.31_... | conditional | flops 2017290240 | bytes 56561976 | solution.py:232
  922.4 17.7 %all-reduce.5 = (f32[32]{0:T(128)S(1)}, f32[32]{0:T(128)S(1)}) all-reduce(f32[32]{0:T(128)S(1)} %get-tuple-element.971, f32[32]{0:T(128)S(1)} %get-tuple-element.972), channel_id=1, replica_groups=mesh['section'=4,'space'=8] {'space'}, use_global_device_ids=true, to_apply=%region_55.55 | all-reduce | flops 64 | bytes 512 | tf_op jit(solution)/shard_map/while/body/eval_jaxpr/psum | solution.py:161
  941.6 8.4 conditional.16
  957.6 115.0 %collective-permute-start.9 = (bf16[6,128,320]{1,2,0:T(8,128)(2,1)}, bf16[6,128,320]{1,2,0:T(8,128)(2,1)S(1)}, u32[]{:S(2)}, u32[]{:S(2)}) collective-permute-start(bf16[6,128,320]{1,2,0:T(8,128)(2,1)} %pad_maximum_fusion.7), channel_id=1, source_target_pairs={{0,24},{1,25},{2,26},{3,27},{4,28},{5,29},{6,30},{7,31}} | collective-permute-start | bytes 1474568 | tf_op jit(solution)/shard_map/while/body/eval_jaxpr/ppermute | solution.py:45
  1076.6 6.7 collective-permute-done.9
  1083.4 3.3 collective-permute-done.8
  1089.7 26.1 %reduce-scatter.2.cloned.1.call-done = bf16[1,4,32,320]{3,2,1,0:T(8,128)(2,1)} async-done(((bf16[1,4,128,320]{3,2,1,0:T(8,128)(2,1)}), bf16[1,4,32,320]{3,2,1,0:T(8,128)(2,1)}) %reduce-scatter.2.cloned.1.call-update) | async-done | bytes 81936 | tf_op jit(solution)/shard_map/reduce_scatter | solution.py:319
  (399 shorter events, 165.0 us)
Async XLA Ops:
  6.5 1109.3 %reduce-scatter.2.cloned.1.call-start = ((), (), s32[]{:S(2)}) async-start(), calls=%async_computation.1 | async-start | bytes 491520 | tf_op jit(solution)/shard_map/reduce_scatter | solution.py:319
  6.5 24.6 %collective-permute-start.10 = (bf16[1,11520,80]{1,2,0:T(8,128)(2,1)}, bf16[1,11520,80]{1,2,0:T(8,128)(2,1)S(1)}, u32[]{:S(2)}, u32[]{:S(2)}) collective-permute-start(bf16[1,11520,80]{1,2,0:T(8,128)(2,1)} %param.35), channel_id=1, source_target_pairs={{0,1},{1,2},{2,3},{3,4},{4,5},{5,6},{6,7},{7,0},{8,9},{9,10},{10,1... | collective-permute-start | bytes 5529608 | tf_op jit(solution)/shard_map/ppermute | solution.py:21
  31.1 1.2 copy-start.10
  32.4 23.6 %collective-permute-start.11 = (bf16[1,11520,80]{1,2,0:T(8,128)(2,1)S(1)}, bf16[1,11520,80]{1,2,0:T(8,128)(2,1)S(1)}, u32[]{:S(2)}, u32[]{:S(2)}) collective-permute-start(bf16[1,11520,80]{1,2,0:T(8,128)(2,1)S(1)} %collective-permute-done.10), channel_id=1, source_target_pairs={{0,1},{1,2},{2,3},{3,4},{4,5},{5,6},{6,7},{7,0},{8,9},{9,10},{10,1... | collective-permute-start | bytes 5529608 | tf_op jit(solution)/shard_map/ppermute | solution.py:21
  56.0 1.2 copy-start.11
  57.2 23.6 %collective-permute-start.12 = (bf16[1,11520,80]{1,2,0:T(8,128)(2,1)S(1)}, bf16[1,11520,80]{1,2,0:T(8,128)(2,1)S(1)}, u32[]{:S(2)}, u32[]{:S(2)}) collective-permute-start(bf16[1,11520,80]{1,2,0:T(8,128)(2,1)S(1)} %collective-permute-done.11), channel_id=1, source_target_pairs={{0,1},{1,2},{2,3},{3,4},{4,5},{5,6},{6,7},{7,0},{8,9},{9,10},{10,1... | collective-permute-start | bytes 5529608 | tf_op jit(solution)/shard_map/ppermute | solution.py:21
  80.9 1.3 copy-start.12
  82.2 23.6 %collective-permute-start.13 = (bf16[1,11520,80]{1,2,0:T(8,128)(2,1)S(1)}, bf16[1,11520,80]{1,2,0:T(8,128)(2,1)S(1)}, u32[]{:S(2)}, u32[]{:S(2)}) collective-permute-start(bf16[1,11520,80]{1,2,0:T(8,128)(2,1)S(1)} %collective-permute-done.12), channel_id=1, source_target_pairs={{0,1},{1,2},{2,3},{3,4},{4,5},{5,6},{6,7},{7,0},{8,9},{9,10},{10,1... | collective-permute-start | bytes 5529608 | tf_op jit(solution)/shard_map/ppermute | solution.py:21
  105.8 1.3 copy-start.13
  107.1 23.6 %collective-permute-start.14 = (bf16[1,11520,80]{1,2,0:T(8,128)(2,1)S(1)}, bf16[1,11520,80]{1,2,0:T(8,128)(2,1)S(1)}, u32[]{:S(2)}, u32[]{:S(2)}) collective-permute-start(bf16[1,11520,80]{1,2,0:T(8,128)(2,1)S(1)} %collective-permute-done.13), channel_id=1, source_target_pairs={{0,1},{1,2},{2,3},{3,4},{4,5},{5,6},{6,7},{7,0},{8,9},{9,10},{10,1... | collective-permute-start | bytes 5529608 | tf_op jit(solution)/shard_map/ppermute | solution.py:21
  130.7 1.2 copy-start.14
  132.0 23.7 %collective-permute-start.15 = (bf16[1,11520,80]{1,2,0:T(8,128)(2,1)S(1)}, bf16[1,11520,80]{1,2,0:T(8,128)(2,1)}, u32[]{:S(2)}, u32[]{:S(2)}) collective-permute-start(bf16[1,11520,80]{1,2,0:T(8,128)(2,1)S(1)} %collective-permute-done.14), channel_id=1, source_target_pairs={{0,1},{1,2},{2,3},{3,4},{4,5},{5,6},{6,7},{7,0},{8,9},{9,10},{10,1... | collective-permute-start | bytes 5529608 | tf_op jit(solution)/shard_map/ppermute | solution.py:21
  155.7 248.1 %collective-permute-start.16 = (bf16[1,11520,80]{1,2,0:T(8,128)(2,1)}, bf16[1,11520,80]{1,2,0:T(8,128)(2,1)}, u32[]{:S(2)}, u32[]{:S(2)}) collective-permute-start(bf16[1,11520,80]{1,2,0:T(8,128)(2,1)} %collective-permute-done.15), channel_id=1, source_target_pairs={{0,1},{1,2},{2,3},{3,4},{4,5},{5,6},{6,7},{7,0},{8,9},{9,10},{10,1... | collective-permute-start | bytes 5529608 | tf_op jit(solution)/shard_map/ppermute | solution.py:21
  465.3 3.0 collective-permute-start
  466.6 3.9 collective-permute-start.1
  468.3 15.1 %copy-start = (bf16[4,128,320]{2,1,0:T(8,128)(2,1)}, bf16[4,128,320]{2,1,0:T(8,128)(2,1)S(1)}, u32[]{:S(2)}) copy-start(bf16[4,128,320]{2,1,0:T(8,128)(2,1)S(1)} %slice_bitcast_fusion.19) | copy-start | bytes 983044 | tf_op jit(solution)/shard_map/while
  477.9 19.4 %collective-permute-start.2 = (bf16[1,40960]{1,0:T(2,128)(2,1)S(1)}, bf16[1,40960]{1,0:T(2,128)(2,1)S(1)}, u32[]{:S(2)}, u32[]{:S(2)}) collective-permute-start(bf16[1,40960]{1,0:T(2,128)(2,1)S(1)} %get-tuple-element.955), channel_id=1, source_target_pairs={{0,1},{1,2},{2,3},{3,4},{4,5},{5,6},{6,7},{8,9},{9,10},{10,11},{11... | collective-permute-start | bytes 245768 | tf_op jit(solution)/shard_map/while/body/eval_jaxpr/ppermute | solution.py:36
  482.1 15.2 %collective-permute-start.3 = (bf16[1,40960]{1,0:T(2,128)(2,1)S(1)}, bf16[1,40960]{1,0:T(2,128)(2,1)S(1)}, u32[]{:S(2)}, u32[]{:S(2)}) collective-permute-start(bf16[1,40960]{1,0:T(2,128)(2,1)S(1)} %get-tuple-element.956), channel_id=1, source_target_pairs={{1,0},{2,1},{3,2},{4,3},{5,4},{6,5},{7,6},{9,8},{10,9},{11,10},{12... | collective-permute-start | bytes 245768 | tf_op jit(solution)/shard_map/while/body/eval_jaxpr/ppermute | solution.py:37
  502.4 3.1 copy-start.16
  526.6 2.6 collective-permute-start.4
  527.9 4.2 collective-permute-start.5
  555.5 3.1 copy-start.18
  571.3 8.9 copy-start.8
  571.6 4.6 collective-permute-start.6
  573.2 4.0 collective-permute-start.7
  578.9 20.0 %collective-permute-start.9 = (bf16[6,128,320]{1,2,0:T(8,128)(2,1)}, bf16[6,128,320]{1,2,0:T(8,128)(2,1)S(1)}, u32[]{:S(2)}, u32[]{:S(2)}) collective-permute-start(bf16[6,128,320]{1,2,0:T(8,128)(2,1)} %pad_maximum_fusion.7), channel_id=1, source_target_pairs={{0,24},{1,25},{2,26},{3,27},{4,28},{5,29},{6,30},{7,31}} | collective-permute-start | bytes 1474568 | tf_op jit(solution)/shard_map/while/body/eval_jaxpr/ppermute | solution.py:45
  586.6 7.2 copy-start.24
  597.6 4.3 collective-permute-start.8
  604.6 5.8 collective-permute-start
  608.8 5.3 collective-permute-start.1
  610.4 14.7 %copy-start = (bf16[4,128,320]{2,1,0:T(8,128)(2,1)}, bf16[4,128,320]{2,1,0:T(8,128)(2,1)S(1)}, u32[]{:S(2)}) copy-start(bf16[4,128,320]{2,1,0:T(8,128)(2,1)S(1)} %slice_bitcast_fusion.19) | copy-start | bytes 983044 | tf_op jit(solution)/shard_map/while
  617.2 22.8 %collective-permute-start.2 = (bf16[1,40960]{1,0:T(2,128)(2,1)S(1)}, bf16[1,40960]{1,0:T(2,128)(2,1)S(1)}, u32[]{:S(2)}, u32[]{:S(2)}) collective-permute-start(bf16[1,40960]{1,0:T(2,128)(2,1)S(1)} %get-tuple-element.955), channel_id=1, source_target_pairs={{0,1},{1,2},{2,3},{3,4},{4,5},{5,6},{6,7},{8,9},{9,10},{10,11},{11... | collective-permute-start | bytes 245768 | tf_op jit(solution)/shard_map/while/body/eval_jaxpr/ppermute | solution.py:36
  623.8 16.2 %collective-permute-start.3 = (bf16[1,40960]{1,0:T(2,128)(2,1)S(1)}, bf16[1,40960]{1,0:T(2,128)(2,1)S(1)}, u32[]{:S(2)}, u32[]{:S(2)}) collective-permute-start(bf16[1,40960]{1,0:T(2,128)(2,1)S(1)} %get-tuple-element.956), channel_id=1, source_target_pairs={{1,0},{2,1},{3,2},{4,3},{5,4},{6,5},{7,6},{9,8},{10,9},{11,10},{12... | collective-permute-start | bytes 245768 | tf_op jit(solution)/shard_map/while/body/eval_jaxpr/ppermute | solution.py:37
  656.8 2.6 collective-permute-start.4
  658.1 4.9 collective-permute-start.5
  691.6 8.9 copy-start.8
  691.9 4.6 collective-permute-start.6
  693.5 4.0 collective-permute-start.7
  699.2 52.6 %collective-permute-start.9 = (bf16[6,128,320]{1,2,0:T(8,128)(2,1)}, bf16[6,128,320]{1,2,0:T(8,128)(2,1)S(1)}, u32[]{:S(2)}, u32[]{:S(2)}) collective-permute-start(bf16[6,128,320]{1,2,0:T(8,128)(2,1)} %pad_maximum_fusion.7), channel_id=1, source_target_pairs={{0,24},{1,25},{2,26},{3,27},{4,28},{5,29},{6,30},{7,31}} | collective-permute-start | bytes 1474568 | tf_op jit(solution)/shard_map/while/body/eval_jaxpr/ppermute | solution.py:45
  702.8 52.3 %collective-permute-start.8 = (bf16[2,64,640]{2,0,1:T(2,128)(2,1)S(1)}, bf16[2,64,640]{2,0,1:T(2,128)(2,1)S(1)}, u32[]{:S(2)}, u32[]{:S(2)}) collective-permute-start(bf16[2,64,640]{2,0,1:T(2,128)(2,1)S(1)} %get-tuple-element.1090), channel_id=1, source_target_pairs={{0,8},{8,16},{16,24},{1,9},{9,17},{17,25},{2,10},{10,18},{18,26},{... | collective-permute-start | bytes 491528 | tf_op jit(solution)/shard_map/while/body/eval_jaxpr/ppermute | solution.py:45
  755.6 5.0 collective-permute-start
  758.9 6.7 collective-permute-start.1
  760.6 16.7 %copy-start = (bf16[4,128,320]{2,1,0:T(8,128)(2,1)}, bf16[4,128,320]{2,1,0:T(8,128)(2,1)S(1)}, u32[]{:S(2)}) copy-start(bf16[4,128,320]{2,1,0:T(8,128)(2,1)S(1)} %slice_bitcast_fusion.19) | copy-start | bytes 983044 | tf_op jit(solution)/shard_map/while
  768.8 21.9 %collective-permute-start.2 = (bf16[1,40960]{1,0:T(2,128)(2,1)S(1)}, bf16[1,40960]{1,0:T(2,128)(2,1)S(1)}, u32[]{:S(2)}, u32[]{:S(2)}) collective-permute-start(bf16[1,40960]{1,0:T(2,128)(2,1)S(1)} %get-tuple-element.955), channel_id=1, source_target_pairs={{0,1},{1,2},{2,3},{3,4},{4,5},{5,6},{6,7},{8,9},{9,10},{10,11},{11... | collective-permute-start | bytes 245768 | tf_op jit(solution)/shard_map/while/body/eval_jaxpr/ppermute | solution.py:36
  775.9 14.8 %collective-permute-start.3 = (bf16[1,40960]{1,0:T(2,128)(2,1)S(1)}, bf16[1,40960]{1,0:T(2,128)(2,1)S(1)}, u32[]{:S(2)}, u32[]{:S(2)}) collective-permute-start(bf16[1,40960]{1,0:T(2,128)(2,1)S(1)} %get-tuple-element.956), channel_id=1, source_target_pairs={{1,0},{2,1},{3,2},{4,3},{5,4},{6,5},{7,6},{9,8},{10,9},{11,10},{12... | collective-permute-start | bytes 245768 | tf_op jit(solution)/shard_map/while/body/eval_jaxpr/ppermute | solution.py:37
  807.3 2.6 collective-permute-start.4
  808.7 4.9 collective-permute-start.5
  842.1 8.9 copy-start.8
  842.4 4.6 collective-permute-start.6
  844.0 4.0 collective-permute-start.7
  849.7 11.7 %collective-permute-start.9 = (bf16[6,128,320]{1,2,0:T(8,128)(2,1)}, bf16[6,128,320]{1,2,0:T(8,128)(2,1)S(1)}, u32[]{:S(2)}, u32[]{:S(2)}) collective-permute-start(bf16[6,128,320]{1,2,0:T(8,128)(2,1)} %pad_maximum_fusion.7), channel_id=1, source_target_pairs={{0,24},{1,25},{2,26},{3,27},{4,28},{5,29},{6,30},{7,31}} | collective-permute-start | bytes 1474568 | tf_op jit(solution)/shard_map/while/body/eval_jaxpr/ppermute | solution.py:45
  853.4 11.4 %collective-permute-start.8 = (bf16[2,64,640]{2,0,1:T(2,128)(2,1)S(1)}, bf16[2,64,640]{2,0,1:T(2,128)(2,1)S(1)}, u32[]{:S(2)}, u32[]{:S(2)}) collective-permute-start(bf16[2,64,640]{2,0,1:T(2,128)(2,1)S(1)} %get-tuple-element.1090), channel_id=1, source_target_pairs={{0,8},{8,16},{16,24},{1,9},{9,17},{17,25},{2,10},{10,18},{18,26},{... | collective-permute-start | bytes 491528 | tf_op jit(solution)/shard_map/while/body/eval_jaxpr/ppermute | solution.py:45
  865.4 5.3 collective-permute-start
  869.0 6.4 collective-permute-start.1
  870.7 14.7 %copy-start = (bf16[4,128,320]{2,1,0:T(8,128)(2,1)}, bf16[4,128,320]{2,1,0:T(8,128)(2,1)S(1)}, u32[]{:S(2)}) copy-start(bf16[4,128,320]{2,1,0:T(8,128)(2,1)S(1)} %slice_bitcast_fusion.19) | copy-start | bytes 983044 | tf_op jit(solution)/shard_map/while
  878.3 20.6 %collective-permute-start.2 = (bf16[1,40960]{1,0:T(2,128)(2,1)S(1)}, bf16[1,40960]{1,0:T(2,128)(2,1)S(1)}, u32[]{:S(2)}, u32[]{:S(2)}) collective-permute-start(bf16[1,40960]{1,0:T(2,128)(2,1)S(1)} %get-tuple-element.955), channel_id=1, source_target_pairs={{0,1},{1,2},{2,3},{3,4},{4,5},{5,6},{6,7},{8,9},{9,10},{10,11},{11... | collective-permute-start | bytes 245768 | tf_op jit(solution)/shard_map/while/body/eval_jaxpr/ppermute | solution.py:36
  884.1 14.9 %collective-permute-start.3 = (bf16[1,40960]{1,0:T(2,128)(2,1)S(1)}, bf16[1,40960]{1,0:T(2,128)(2,1)S(1)}, u32[]{:S(2)}, u32[]{:S(2)}) collective-permute-start(bf16[1,40960]{1,0:T(2,128)(2,1)S(1)} %get-tuple-element.956), channel_id=1, source_target_pairs={{1,0},{2,1},{3,2},{4,3},{5,4},{6,5},{7,6},{9,8},{10,9},{11,10},{12... | collective-permute-start | bytes 245768 | tf_op jit(solution)/shard_map/while/body/eval_jaxpr/ppermute | solution.py:37
  915.7 2.6 collective-permute-start.4
  917.0 4.8 collective-permute-start.5
  950.1 122.6 %copy-start.8 = (bf16[1,4,128,320]{2,3,1,0:T(8,128)(2,1)S(1)}, bf16[1,4,128,320]{2,3,1,0:T(8,128)(2,1)}, u32[]{:S(2)}) copy-start(bf16[1,4,128,320]{2,3,1,0:T(8,128)(2,1)} %get-tuple-element.1063) | copy-start | bytes 983044 | tf_op jit(solution)/shard_map/while
  950.4 4.6 collective-permute-start.6
  952.0 4.0 collective-permute-start.7
  957.6 125.7 %collective-permute-start.9 = (bf16[6,128,320]{1,2,0:T(8,128)(2,1)}, bf16[6,128,320]{1,2,0:T(8,128)(2,1)S(1)}, u32[]{:S(2)}, u32[]{:S(2)}) collective-permute-start(bf16[6,128,320]{1,2,0:T(8,128)(2,1)} %pad_maximum_fusion.7), channel_id=1, source_target_pairs={{0,24},{1,25},{2,26},{3,27},{4,28},{5,29},{6,30},{7,31}} | collective-permute-start | bytes 1474568 | tf_op jit(solution)/shard_map/while/body/eval_jaxpr/ppermute | solution.py:45
  1075.3 11.4 %collective-permute-start.8 = (bf16[2,64,640]{2,0,1:T(2,128)(2,1)S(1)}, bf16[2,64,640]{2,0,1:T(2,128)(2,1)S(1)}, u32[]{:S(2)}, u32[]{:S(2)}) collective-permute-start(bf16[2,64,640]{2,0,1:T(2,128)(2,1)S(1)} %get-tuple-element.1090), channel_id=1, source_target_pairs={{0,8},{8,16},{16,24},{1,9},{9,17},{17,25},{2,10},{10,18},{18,26},{... | collective-permute-start | bytes 491528 | tf_op jit(solution)/shard_map/while/body/eval_jaxpr/ppermute | solution.py:45
  (5 other events, 3.9 us)
Sparse Core Ops, SparseCore 0:
  1089.9 25.9 reduce-scatter.1
